TPU v7x, 32 devices: a whole 2x2x4 slice. The times are simulated.
32 devices in a mesh: row: 8 (over z, y), col: 4 (over x, core).
Axes of the slice: x: 2, y: 2, z: 4, core: 2. Of those that a mesh axis runs over, the one named last changes fastest.
Arguments:
- start_block: float32 [64, 16, 128], P(('row', 'col')), may hold values from -6 to 6
- blocks: float32 [8, 4, 58, 128, 128], P('row', 'col'), as said below
- slot_row: int32 [8, 4, 58], P('row', 'col'), may hold values from 0 to 7, as said below
- slot_col: int32 [8, 4, 58], P('row', 'col'), may hold values from 0 to 15, as said below
- counts: int32 [8, 4], P('row', 'col'), may hold values from 34 to 58, as said below
Outputs:
- alphas: float32 [2, 16, 16], replicated
- betas: float32 [2, 16, 16], replicated
- next_block: float32 [64, 16, 128], P(('row', 'col'))
Inputs may be any that keep to these rules, and one draw needn't show every extreme that they name: `blocks`: over all cells the live slots list each nonzero block of a symmetric matrix exactly once: block (J, I) is listed exactly when (I, J) is, holding its transpose. Slots at or past a cell's count hold finite values that are no part of H. `counts`: live slots of a cell come first; in every draw some cell has all 58 slots live. `slot_row`: for live slots, the block row within the cell's row group of 8 block rows. `slot_col`: for live slots, the position within the cell's column group of 16 block columns, as in the first step.
All inputs are finite; a program needn't handle non-finite values.
Results may differ from a plain program's by a relative error of at most 0.0003.
Values sent between devices are 32-bit elements; how exact they have to be, the bound alone decides.
A program may use at most 64 MiB of HBM per device.

v0:
```python
import functools

import jax
import jax.numpy as jnp
from jax import lax
from jax.experimental import pallas as pl
from jax.experimental.pallas import tpu as pltpu
from jax.sharding import PartitionSpec as P

HIGHEST = lax.Precision.HIGHEST
F32 = jnp.float32
BF16 = jnp.bfloat16
NN = (((1,), (0,)), ((), ()))
NT = (((1,), (1,)), ((), ()))
TN = (((0,), (0,)), ((), ()))


def dot(left, right, dims=NN):
    return lax.dot_general(left, right, dims, precision=HIGHEST, preferred_element_type=F32)


def factor(gram):
    n = gram.shape[0]
    rows = lax.broadcasted_iota(jnp.int32, (n, n), 0)
    cols = lax.broadcasted_iota(jnp.int32, (n, n), 1)
    work = jnp.concatenate([gram, (rows == cols).astype(F32)], axis=1)
    index = lax.broadcasted_iota(jnp.int32, (n, 2 * n), 0)
    for j in range(n - 1):
        ratio = work[j : j + 1, :] / work[j : j + 1, j : j + 1]
        work = work - jnp.where(index > j, work[:, j : j + 1], 0.0) * ratio
    upper = work[:, :n]
    pivots = jnp.sum(jnp.where(rows == cols, upper, 0.0), axis=1, keepdims=True)
    scale = 1.0 / jnp.sqrt(pivots)
    return jnp.where(rows <= cols, upper, 0.0) * scale, work[:, n:] * scale


def pack(gram):
    quarter = gram.shape[0] // 4
    return jnp.concatenate([gram[i * quarter : (i + 1) * quarter] for i in range(4)], axis=1)


def unpack(packed):
    width = packed.shape[1] // 4
    return jnp.concatenate([packed[:, i * width : (i + 1) * width] for i in range(4)], axis=0)


def kernel(
    nr, nc, group, total,
    rows_hbm, cols_hbm, counts_hbm, start_ref, blocks_ref,
    packed_ref,
    tiles, weights, expanded, gat, xhi, xlo, part, scat, ybuf, gsend, grow, gcol_send, gcol,
    rows_ref, cols_ref, counts_ref,
    load_sem, row_send, row_recv, col_send, col_recv, gr_send, gr_recv, gc_send, gc_recv,
):
    me_r = lax.axis_index("row")
    me_c = lax.axis_index("col")
    capacity = tiles.shape[0]
    piece, k, orb = start_ref.shape
    local_rows = nc * piece

    loads = [
        pltpu.make_async_copy(start_ref, gat.at[0, me_r], load_sem.at[0]),
        pltpu.make_async_copy(rows_hbm, rows_ref, load_sem.at[1]),
        pltpu.make_async_copy(cols_hbm, cols_ref, load_sem.at[2]),
        pltpu.make_async_copy(counts_hbm, counts_ref, load_sem.at[3]),
        pltpu.make_async_copy(blocks_ref, tiles, load_sem.at[4]),
    ]

    def row_peer(d):
        return (lax.rem(me_r + d, nr), me_c)

    def col_peer(d):
        return (me_r, lax.rem(me_c + d, nc))

    barrier = pltpu.get_barrier_semaphore()
    for d in range(1, nr):
        pl.semaphore_signal(barrier, inc=1, device_id=row_peer(d), device_id_type=pl.DeviceIdType.MESH)
    for d in range(1, nc):
        pl.semaphore_signal(barrier, inc=1, device_id=col_peer(d), device_id_type=pl.DeviceIdType.MESH)
    for load in loads:
        load.start()
    pl.semaphore_wait(barrier, nr + nc - 2)

    def spread_row(src, dst, send, recv, step):
        copies = []
        for d in range(1, nr):
            copy = pltpu.make_async_remote_copy(
                src_ref=src, dst_ref=dst.at[me_r],
                send_sem=send.at[step, d], recv_sem=recv.at[step, d],
                device_id=row_peer(d), device_id_type=pl.DeviceIdType.MESH,
            )
            copy.start()
            copies.append(copy)
        return copies

    def spread_col(src, dst, send, recv, step, scatter):
        copies = []
        for d in range(1, nc):
            peer = lax.rem(me_c + d, nc)
            copy = pltpu.make_async_remote_copy(
                src_ref=src.at[peer] if scatter else src, dst_ref=dst.at[me_c],
                send_sem=send.at[step, d], recv_sem=recv.at[step, d],
                device_id=(me_r, peer), device_id_type=pl.DeviceIdType.MESH,
            )
            copy.start()
            copies.append(copy)
        return copies

    def received(copies):
        for copy in copies:
            copy.wait_recv()

    def cat(value):
        return jnp.concatenate([value[p] for p in range(piece)], axis=1)

    pending = []
    first = spread_row(start_ref, gat.at[0], row_send, row_recv, 0)
    pending += first
    def mean_start(step, gram):
        gsend[step] = pack(gram) * (1.0 / total)
        return spread_row(gsend.at[step], grow.at[step], gr_send, gr_recv, step)

    def mean_row(step, copies):
        received(copies)
        grow[step, pl.ds(me_r, 1)] = gsend[step][None]
        value = grow[step, 0]
        for r in range(1, nr):
            value = value + grow[step, r]
        return value

    def mean_column(step, value):
        gcol_send[step] = value
        return spread_col(gcol_send.at[step], gcol.at[step], gc_send, gc_recv, step, False)

    def cat_group(step):
        return jnp.concatenate([gat[step, r, p] for r in range(nr) for p in range(piece)], axis=1)

    def mean_end(step, copies):
        received(copies)
        gcol[step, pl.ds(me_c, 1)] = gcol_send[step][None]
        value = gcol[step, 0]
        for c in range(1, nc):
            value = value + gcol[step, c]
        return unpack(value)

    loads[0].wait()
    s_cat = cat(gat[0, me_r])
    for load in loads[1:]:
        load.wait()
    count = counts_ref[0, 0]

    def split_tile(s, carry):
        tile = lax.select(jnp.broadcast_to(s < count, (orb, orb)), tiles[s], jnp.zeros((orb, orb), F32))
        high = tile.astype(BF16)
        weights[s, :orb] = high
        weights[s, orb:] = (tile - high.astype(F32)).astype(BF16)
        return carry

    lax.fori_loop(0, capacity, split_tile, 0, unroll=2)

    half = local_rows * k

    def operate(step):
        def split_vectors(q, carry):
            for p in range(piece):
                value = gat[step, q, p]
                high = value.astype(BF16)
                xhi[q * piece + p] = high
                xlo[q * piece + p] = (value - high.astype(F32)).astype(BF16)
            return carry

        lax.fori_loop(0, nr, split_vectors, 0, unroll=nr <= 8)

        def chunk(base):
            for t in range(group):
                s = base + t
                col = jnp.clip(lax.select(s < count, cols_ref[s], 0), 0, nr * piece - 1)
                row = rows_ref[s]
                high, low = xhi[col], xlo[col]
                zero = jnp.zeros_like(high)
                for r in range(local_rows):
                    hit = row == r
                    expanded[r * k : (r + 1) * k, t * orb : (t + 1) * orb] = lax.select(hit, high, zero)
                    expanded[half + r * k : half + (r + 1) * k, t * orb : (t + 1) * orb] = lax.select(hit, low, zero)
            flat = jnp.concatenate([weights[base + t] for t in range(group)], axis=1)
            return lax.dot_general(expanded[...], flat, NT, preferred_element_type=F32)

        if capacity == group:
            acc = chunk(0)
        else:
            acc = lax.fori_loop(
                0, capacity // group, lambda g, a: a + chunk(g * group),
                jnp.zeros((2 * half, 2 * orb), F32),
            )
        out = acc[:half, :orb] + acc[:half, orb:] + acc[half:, :orb]
        for r in range(local_rows):
            part[step, r // piece, r % piece] = out[r * k : (r + 1) * k]
        return spread_col(part.at[step], scat.at[step], col_send, col_recv, step, True)

    def reduced(step, copies):
        received(copies)
        own = part[step, me_c]
        for d in range(1, nc):
            own = own + scat[step, lax.rem(me_c + d, nc)]
        return own

    received(first)
    s_all = cat_group(0)
    ss = dot(s_all, s_all, NT)
    ss = jnp.concatenate([ss, ss], axis=1)
    middle_s = mean_column(0, pack(jnp.concatenate([ss, ss], axis=0)) * (1.0 / total))
    pending += middle_s
    scatter0 = operate(0)
    pending += scatter0
    _, inv0 = factor(mean_end(0, middle_s)[:k, :k])
    v1 = dot(inv0, s_cat)
    v1_all = dot(inv0, cat_group(0))
    y_raw = reduced(0, scatter0)
    ybuf[...] = y_raw
    gat[1, pl.ds(me_r, 1)] = y_raw[None]
    second = spread_row(ybuf, gat.at[1], row_send, row_recv, 1)
    pending += second
    hv1 = dot(inv0, cat(y_raw))
    received(second)
    both = jnp.concatenate([v1_all, dot(inv0, cat_group(1))], axis=0)
    middle0 = mean_column(1, pack(dot(both, both, NT)) * (1.0 / total))
    pending += middle0
    scatter1 = operate(1)
    pending += scatter1
    gram = mean_end(1, middle0)
    q1, alpha1, yy1 = gram[:k, :k], gram[:k, k:], gram[k:, k:]
    beta1, inv1 = factor(yy1 - dot(alpha1, alpha1, TN) - dot(alpha1, alpha1 - dot(q1, alpha1), TN))
    v2 = dot(inv1, hv1 - dot(alpha1, v1, TN))
    known = dot(beta1, v1)
    shift = dot(dot(inv1, alpha1, NT), hv1)
    lead = dot(inv1, inv0)
    y2 = dot(lead, cat(reduced(1, scatter1))) - shift
    w2 = y2 - known
    both = jnp.concatenate([v2, w2], axis=0)
    grams = dot(both, jnp.concatenate([both, y2], axis=0), NT)
    top = grams[:k, : 2 * k]
    low = jnp.concatenate([grams[:k, 2 * k :], grams[k:, k : 2 * k]], axis=1)
    mean1 = mean_start(0, jnp.concatenate([top, low], axis=0))
    pending += mean1
    middle1 = mean_column(2, mean_row(0, mean1))
    pending += middle1
    gram = mean_end(2, middle1)
    qq, pw, alpha2, ww = gram[:k, :k], gram[:k, k:], gram[k:, :k], gram[k:, k:]
    rest = pw - dot(qq, alpha2)
    beta2, inv2 = factor(ww - dot(pw, alpha2, TN) - dot(alpha2, rest, TN))
    out = dot(inv2, w2 - dot(alpha2, v2, TN))
    for p in range(piece):
        packed_ref[p, :, :orb] = out[:, p * orb : (p + 1) * orb]
    packed_ref[piece, :, : 4 * k] = jnp.concatenate([alpha1, alpha2, beta1, beta2], axis=1)
    for copy in pending:
        copy.wait_send()


def finish(packed_ref, alphas_ref, betas_ref, next_ref):
    piece, k, _ = next_ref.shape
    small = packed_ref[piece]
    for step in range(2):
        alphas_ref[step] = small[:, step * k : (step + 1) * k]
        betas_ref[step] = small[:, (2 + step) * k : (3 + step) * k]
    next_ref[...] = packed_ref[:piece]


def on_device(nr, nc, start_block, blocks, slot_row, slot_col, counts):
    capacity = blocks.shape[2]
    orb = blocks.shape[3]
    piece, k, _ = start_block.shape
    local_rows = nc * piece
    total = float(piece * nr * nc * orb)
    group = max(g for g in range(1, 65) if capacity % g == 0 and g * local_rows * k <= 64 * 128)
    vmem = pl.BlockSpec(memory_space=pltpu.VMEM)
    dma = pltpu.SemaphoreType.DMA
    width = 4 * 2 * k
    height = 2 * k // 4
    packed = pl.pallas_call(
        functools.partial(kernel, nr, nc, group, total),
        out_shape=jax.ShapeDtypeStruct((piece + 1, k, orb), F32),
        in_specs=[pl.BlockSpec(memory_space=pltpu.HBM)] * 5,
        out_specs=vmem,
        scratch_shapes=[
            pltpu.VMEM((capacity, orb, orb), F32),
            pltpu.VMEM((capacity, 2 * orb, orb), BF16),
            pltpu.VMEM((2 * local_rows * k, group * orb), BF16),
            pltpu.VMEM((2, nr, piece, k, orb), F32),
            pltpu.VMEM((nr * piece, k, orb), BF16),
            pltpu.VMEM((nr * piece, k, orb), BF16),
            pltpu.VMEM((2, nc, piece, k, orb), F32),
            pltpu.VMEM((2, nc, piece, k, orb), F32),
            pltpu.VMEM((piece, k, orb), F32),
            pltpu.VMEM((1, height, width), F32),
            pltpu.VMEM((1, nr, height, width), F32),
            pltpu.VMEM((3, height, width), F32),
            pltpu.VMEM((3, nc, height, width), F32),
            pltpu.SMEM((capacity,), jnp.int32),
            pltpu.SMEM((capacity,), jnp.int32),
            pltpu.SMEM((1, 1), jnp.int32),
            dma((5,)),
            dma((2, nr)), dma((2, nr)),
            dma((2, nc)), dma((2, nc)),
            dma((1, nr)), dma((1, nr)),
            dma((3, nc)), dma((3, nc)),
        ],
        compiler_params=pltpu.CompilerParams(
            collective_id=0, has_side_effects=True, vmem_limit_bytes=61 << 20
        ),
    )(slot_row[0, 0], slot_col[0, 0], counts, start_block, blocks[0, 0])
    return pl.pallas_call(
        finish,
        out_shape=(
            jax.ShapeDtypeStruct((2, k, k), F32),
            jax.ShapeDtypeStruct((2, k, k), F32),
            jax.ShapeDtypeStruct((piece, k, orb), F32),
        ),
        in_specs=[vmem],
        out_specs=(vmem, vmem, vmem),
    )(packed)


def solution(mesh):
    placed = (
        P(("row", "col"), None, None),
        P("row", "col", None, None, None),
        P("row", "col", None),
        P("row", "col", None),
        P("row", "col"),
    )
    return jax.shard_map(
        functools.partial(on_device, mesh.shape["row"], mesh.shape["col"]),
        mesh=mesh,
        in_specs=placed,
        out_specs=(P(), P(), P(("row", "col"), None, None)),
        check_vma=False,
    )
```

profile of v0, /device:TPU:0, one launch (start us, length us, event | category | flops | bytes accessed | tf_op | source)
XLA Modules:
  0.0 40.8 jit_solution(2051687379414460784)
XLA Ops:
  1.3 38.1 %shard_map.76.packed_ref = f32[3,16,128]{2,1,0:T(8,128)} custom-call(s32[58]{0:T(128)} %bitcast.4, s32[58]{0:T(128)} %bitcast.5, s32[1,1]{1,0:T(1,128)S(6)} %copy.8.counts_hbm, f32[2,16,128]{2,1,0:T(8,128)} %start_ref.1, f32[58,128,128]{2,1,0:T(8,128)} %bitcast.3), custom_call_target="tpu_custom_call" | custom-call | tf_op jit(solution)/shard_map/pallas_call | solution.py:279
  39.4 1.4 %shard_map.77 = (f32[2,16,16]{2,1,0:T(8,128)}, f32[2,16,16]{2,1,0:T(8,128)}, f32[2,16,128]{2,1,0:T(8,128)}) custom-call(f32[3,16,128]{2,1,0:T(8,128)} %shard_map.76.packed_ref), custom_call_target="tpu_custom_call" | custom-call | tf_op jit(solution)/shard_map/pallas_call | solution.py:311
where the time goes:
time: 41 us; the launch traced here: 40.8 us
  Pallas kernels  39.5 us (96%)
  between operations  1.29 us (3%)
    pallas_call x1, Pallas kernels, on_device(): pl.pallas_call(functools.partial(kernel, nr, nc, group, total), out_shape...  38.1 us
    pallas_call x1, Pallas kernels, on_device(): pl.pallas_call(finish, out_shape=(jax.ShapeDtypeStruct((2, k, k), F32), j...  1.43 us

commit v1 on v0

v1 whole, which is shorter than its diff:
```python
import functools

import jax
import jax.numpy as jnp
from jax import lax
from jax.experimental import pallas as pl
from jax.experimental.pallas import tpu as pltpu
from jax.sharding import PartitionSpec as P

HIGHEST = lax.Precision.HIGHEST
F32 = jnp.float32
BF16 = jnp.bfloat16
NN = (((1,), (0,)), ((), ()))
NT = (((1,), (1,)), ((), ()))
TN = (((0,), (0,)), ((), ()))


def dot(left, right, dims=NN):
    return lax.dot_general(left, right, dims, precision=HIGHEST, preferred_element_type=F32)


def factor(gram):
    n = gram.shape[0]
    rows = lax.broadcasted_iota(jnp.int32, (n, n), 0)
    cols = lax.broadcasted_iota(jnp.int32, (n, n), 1)
    work = jnp.concatenate([gram, (rows == cols).astype(F32)], axis=1)
    index = lax.broadcasted_iota(jnp.int32, (n, 2 * n), 0)
    spread = [jnp.broadcast_to(gram[:, j : j + 1], (n, 2 * n)) for j in range(n)]
    for j in range(n - 1):
        ratio = spread[j] / spread[j][j : j + 1]
        work = work - jnp.where(index > j, ratio, 0.0) * work[j : j + 1]
        for i in range(j + 1, n):
            spread[i] = spread[i] - ratio * spread[i][j : j + 1]
    pivots = jnp.concatenate([spread[j][j : j + 1] for j in range(n)], axis=0)
    scaled = work * (1.0 / jnp.sqrt(pivots))
    return jnp.where(rows <= cols, scaled[:, :n], 0.0), scaled[:, n:]


def pack(gram):
    quarter = gram.shape[0] // 4
    return jnp.concatenate([gram[i * quarter : (i + 1) * quarter] for i in range(4)], axis=1)


def unpack(packed):
    width = packed.shape[1] // 4
    return jnp.concatenate([packed[:, i * width : (i + 1) * width] for i in range(4)], axis=0)


def partners(size, me):
    if size & (size - 1):
        return [(lax.rem(me + d, size), lax.rem(me + size - d, size)) for d in range(size - 1, 0, -1)]
    pairs = []
    for mask in range(size - 1, 0, -1):
        other, bit = me, 1
        while bit < size:
            if mask & bit:
                other = other + bit - 2 * bit * lax.rem(me // bit, 2)
            bit *= 2
        pairs.append((other, other))
    return pairs


def kernel(
    nr, nc, group, total,
    rows_hbm, cols_hbm, counts_hbm, start_ref, blocks_ref,
    packed_ref,
    tiles, weights, gat, xs, part, scat, ybuf, gsend, grow, gcol_send, gcol,
    rows_ref, cols_ref, counts_ref,
    load_sem, row_send, row_recv, col_send, col_recv, gr_send, gr_recv, gc_send, gc_recv,
):
    me_r = lax.axis_index("row")
    me_c = lax.axis_index("col")
    capacity = tiles.shape[0]
    piece, k, orb = start_ref.shape
    local_rows = nc * piece
    row_pairs = partners(nr, me_r)
    col_pairs = partners(nc, me_c)

    loads = [
        pltpu.make_async_copy(start_ref, gat.at[0, me_r], load_sem.at[0]),
        pltpu.make_async_copy(rows_hbm, rows_ref, load_sem.at[1]),
        pltpu.make_async_copy(cols_hbm, cols_ref, load_sem.at[2]),
        pltpu.make_async_copy(counts_hbm, counts_ref, load_sem.at[3]),
        pltpu.make_async_copy(blocks_ref, tiles, load_sem.at[4]),
    ]

    barrier = pltpu.get_barrier_semaphore()
    for to, _ in row_pairs:
        pl.semaphore_signal(barrier, inc=1, device_id=(to, me_c), device_id_type=pl.DeviceIdType.MESH)
    for to, _ in col_pairs:
        pl.semaphore_signal(barrier, inc=1, device_id=(me_r, to), device_id_type=pl.DeviceIdType.MESH)
    for load in loads:
        load.start()
    loads[0].wait()
    pl.semaphore_wait(barrier, nr + nc - 2)

    def spread_row(src, dst, send, recv, step):
        copies = []
        for d, (to, _) in enumerate(row_pairs):
            copy = pltpu.make_async_remote_copy(
                src_ref=src, dst_ref=dst.at[me_r],
                send_sem=send.at[step, d], recv_sem=recv.at[step, d],
                device_id=(to, me_c), device_id_type=pl.DeviceIdType.MESH,
            )
            copy.start()
            copies.append(copy)
        return copies

    def spread_col(src, dst, send, recv, step, scatter):
        copies = []
        for d, (to, _) in enumerate(col_pairs):
            copy = pltpu.make_async_remote_copy(
                src_ref=src.at[to] if scatter else src, dst_ref=dst.at[me_c],
                send_sem=send.at[step, d], recv_sem=recv.at[step, d],
                device_id=(me_r, to), device_id_type=pl.DeviceIdType.MESH,
            )
            copy.start()
            copies.append(copy)
        return copies

    def received(copies):
        for copy in copies:
            copy.wait_recv()

    def cat(value):
        return jnp.concatenate([value[p] for p in range(piece)], axis=1)

    def mean_start(step, gram):
        gsend[step] = pack(gram) * (1.0 / total)
        return spread_row(gsend.at[step], grow.at[step], gr_send, gr_recv, step)

    def mean_row(step, copies):
        received(copies)
        grow[step, pl.ds(me_r, 1)] = gsend[step][None]
        value = grow[step, 0]
        for r in range(1, nr):
            value = value + grow[step, r]
        return value

    def mean_column(step, value):
        gcol_send[step] = value
        return spread_col(gcol_send.at[step], gcol.at[step], gc_send, gc_recv, step, False)

    def mean_end(step, copies):
        received(copies)
        gcol[step, pl.ds(me_c, 1)] = gcol_send[step][None]
        value = gcol[step, 0]
        for c in range(1, nc):
            value = value + gcol[step, c]
        return unpack(value)

    def split_vectors(step, q):
        for p in range(piece):
            value = gat[step, q, p]
            high = value.astype(BF16)
            xs[q * piece + p, :k] = high
            xs[q * piece + p, k:] = (value - high.astype(F32)).astype(BF16)

    def operate(step):
        def slot(s, accs):
            live = s < count
            col = jnp.clip(lax.select(live, cols_ref[s], 0), 0, nr * piece - 1)
            row = lax.select(live, rows_ref[s], -1)
            prod = lax.dot_general(xs[col], weights[s], NT, preferred_element_type=F32)
            prod = prod[:k, :orb] + prod[:k, orb:] + prod[k:, :orb]
            zero = jnp.zeros_like(prod)
            return [acc + lax.select(row == r, prod, zero) for r, acc in enumerate(accs)]

        accs = [jnp.zeros((k, orb), F32)] * local_rows
        if capacity == group:
            for s in range(capacity):
                accs = slot(s, accs)
        else:
            def chunk(g, accs):
                for t in range(group):
                    accs = slot(g * group + t, accs)
                return accs

            accs = lax.fori_loop(0, capacity // group, chunk, accs)
        for r in range(local_rows):
            part[step, r // piece, r % piece] = accs[r]
        return spread_col(part.at[step], scat.at[step], col_send, col_recv, step, True)

    def reduced(step, copies):
        received(copies)
        own = part[step, me_c]
        for _, other in col_pairs:
            own = own + scat[step, other]
        return own

    pending = []
    first = spread_row(gat.at[0, me_r], gat.at[0], row_send, row_recv, 0)
    pending += first
    for load in loads[1:]:
        load.wait()
    count = counts_ref[0, 0]

    def split_tile(s, carry):
        tile = tiles[s]
        high = tile.astype(BF16)
        weights[s, :orb] = high
        weights[s, orb:] = (tile - high.astype(F32)).astype(BF16)
        return carry

    lax.fori_loop(0, capacity, split_tile, 0, unroll=2)
    split_vectors(0, me_r)
    for copy, (_, other) in list(zip(first, row_pairs))[::-1]:
        copy.wait_recv()
        split_vectors(0, other)
    scatter0 = operate(0)
    pending += scatter0
    s_all = jnp.concatenate([gat[0, r, p] for r in range(nr) for p in range(piece)], axis=1)
    ss = dot(s_all, s_all, NT)
    ss = jnp.concatenate([ss, ss], axis=1)
    middle_s = mean_column(0, pack(jnp.concatenate([ss, ss], axis=0)) * (1.0 / total))
    pending += middle_s
    y_raw = reduced(0, scatter0)
    ybuf[...] = y_raw
    gat[1, pl.ds(me_r, 1)] = y_raw[None]
    second = spread_row(ybuf, gat.at[1], row_send, row_recv, 1)
    pending += second
    _, inv0 = factor(mean_end(0, middle_s)[:k, :k])
    v1 = dot(inv0, cat(gat[0, me_r]))
    hv1 = dot(inv0, cat(y_raw))

    def gram_of(q, left, right):
        both = jnp.concatenate([left, right], axis=0)
        return dot(both, both, NT)

    split_vectors(1, me_r)
    both = gram_of(me_r, v1, hv1)
    for copy, (_, other) in list(zip(second, row_pairs))[::-1]:
        left = dot(inv0, cat(gat[0, other]))
        copy.wait_recv()
        split_vectors(1, other)
        both = both + gram_of(other, left, dot(inv0, cat(gat[1, other])))
    middle0 = mean_column(1, pack(both) * (1.0 / total))
    pending += middle0
    scatter1 = operate(1)
    pending += scatter1
    gram = mean_end(1, middle0)
    q1, alpha1, yy1 = gram[:k, :k], gram[:k, k:], gram[k:, k:]
    beta1, inv1 = factor(yy1 - dot(alpha1, alpha1, TN) - dot(alpha1, alpha1 - dot(q1, alpha1), TN))
    v2 = dot(inv1, hv1 - dot(alpha1, v1, TN))
    known = dot(beta1, v1)
    shift = dot(dot(inv1, alpha1, NT), hv1)
    lead = dot(inv1, inv0)
    y2 = dot(lead, cat(reduced(1, scatter1))) - shift
    w2 = y2 - known
    both = jnp.concatenate([v2, w2], axis=0)
    grams = dot(both, jnp.concatenate([both, y2], axis=0), NT)
    top = grams[:k, : 2 * k]
    low = jnp.concatenate([grams[:k, 2 * k :], grams[k:, k : 2 * k]], axis=1)
    mean1 = mean_start(0, jnp.concatenate([top, low], axis=0))
    pending += mean1
    middle1 = mean_column(2, mean_row(0, mean1))
    pending += middle1
    gram = mean_end(2, middle1)
    qq, pw, alpha2, ww = gram[:k, :k], gram[:k, k:], gram[k:, :k], gram[k:, k:]
    rest = pw - dot(qq, alpha2)
    beta2, inv2 = factor(ww - dot(pw, alpha2, TN) - dot(alpha2, rest, TN))
    out = dot(inv2, w2 - dot(alpha2, v2, TN))
    for p in range(piece):
        packed_ref[p, :, :orb] = out[:, p * orb : (p + 1) * orb]
    packed_ref[piece, :, : 4 * k] = jnp.concatenate([alpha1, alpha2, beta1, beta2], axis=1)
    for copy in pending:
        copy.wait_send()


def finish(packed_ref, alphas_ref, betas_ref, next_ref):
    piece, k, _ = next_ref.shape
    small = packed_ref[piece]
    for step in range(2):
        alphas_ref[step] = small[:, step * k : (step + 1) * k]
        betas_ref[step] = small[:, (2 + step) * k : (3 + step) * k]
    next_ref[...] = packed_ref[:piece]


def on_device(nr, nc, start_block, blocks, slot_row, slot_col, counts):
    capacity = blocks.shape[2]
    orb = blocks.shape[3]
    piece, k, _ = start_block.shape
    local_rows = nc * piece
    total = float(piece * nr * nc * orb)
    group = max(g for g in range(1, 65) if capacity % g == 0)
    vmem = pl.BlockSpec(memory_space=pltpu.VMEM)
    dma = pltpu.SemaphoreType.DMA
    width = 4 * 2 * k
    height = 2 * k // 4
    packed = pl.pallas_call(
        functools.partial(kernel, nr, nc, group, total),
        out_shape=pltpu.VMEM((piece + 1, k, orb), F32),
        in_specs=[pl.BlockSpec(memory_space=pltpu.HBM)] * 5,
        out_specs=vmem,
        scratch_shapes=[
            pltpu.VMEM((capacity, orb, orb), F32),
            pltpu.VMEM((capacity, 2 * orb, orb), BF16),
            pltpu.VMEM((2, nr, piece, k, orb), F32),
            pltpu.VMEM((nr * piece, 2 * k, orb), BF16),
            pltpu.VMEM((2, nc, piece, k, orb), F32),
            pltpu.VMEM((2, nc, piece, k, orb), F32),
            pltpu.VMEM((piece, k, orb), F32),
            pltpu.VMEM((1, height, width), F32),
            pltpu.VMEM((1, nr, height, width), F32),
            pltpu.VMEM((3, height, width), F32),
            pltpu.VMEM((3, nc, height, width), F32),
            pltpu.SMEM((capacity,), jnp.int32),
            pltpu.SMEM((capacity,), jnp.int32),
            pltpu.SMEM((1, 1), jnp.int32),
            dma((5,)),
            dma((2, nr)), dma((2, nr)),
            dma((2, nc)), dma((2, nc)),
            dma((1, nr)), dma((1, nr)),
            dma((3, nc)), dma((3, nc)),
        ],
        compiler_params=pltpu.CompilerParams(
            collective_id=0, has_side_effects=True, vmem_limit_bytes=56 << 20
        ),
    )(slot_row[0, 0], slot_col[0, 0], counts, start_block, blocks[0, 0])
    return pl.pallas_call(
        finish,
        out_shape=(
            jax.ShapeDtypeStruct((2, k, k), F32),
            jax.ShapeDtypeStruct((2, k, k), F32),
            jax.ShapeDtypeStruct((piece, k, orb), F32),
        ),
        in_specs=[vmem],
        out_specs=(vmem, vmem, vmem),
    )(pltpu.with_memory_space_constraint(packed, pltpu.VMEM))


def solution(mesh):
    placed = (
        P(("row", "col"), None, None),
        P("row", "col", None, None, None),
        P("row", "col", None),
        P("row", "col", None),
        P("row", "col"),
    )
    return jax.shard_map(
        functools.partial(on_device, mesh.shape["row"], mesh.shape["col"]),
        mesh=mesh,
        in_specs=placed,
        out_specs=(P(), P(), P(("row", "col"), None, None)),
        check_vma=False,
    )
```

time: 41 us -> 36.1 us (0.88)
  Pallas kernels: 39.5 us -> 34.5 us
    pallas_call x1, Pallas kernels: 38.1 us -> 33.8 us  [on_device(): pl.pallas_call(functools.partial(kernel, nr, nc, group, total), out_shape...]
    pallas_call x1, Pallas kernels: 1.43 us -> 0.69 us  [on_device(): pl.pallas_call(finish, out_shape=(jax.ShapeDtypeStruct((2, k, k), F32), j...]
where the time goes in v1:
time: 36.1 us; the launch traced here: 35.8 us
  Pallas kernels  34.5 us (96%)
  between operations  1.29 us (4%)
    pallas_call x1, Pallas kernels, on_device(): pl.pallas_call(functools.partial(kernel, nr, nc, group, total), out_shape...  33.8 us

profile of v1, /device:TPU:0, one launch (start us, length us, event | category | flops | bytes accessed | tf_op | source)
XLA Modules:
  0.0 35.8 jit_solution(13688783579631805886)
XLA Ops:
  1.3 33.8 %shard_map.76.packed_ref = f32[3,16,128]{2,1,0:T(8,128)S(1)} custom-call(s32[58]{0:T(128)} %bitcast.4, s32[58]{0:T(128)} %bitcast.5, s32[1,1]{1,0:T(1,128)S(6)} %copy.8.counts_hbm, f32[2,16,128]{2,1,0:T(8,128)} %start_ref.1, f32[58,128,128]{2,1,0:T(8,128)} %bitcast.3), custom_call_target="tpu_custom_call" | custom-call | tf_op jit(solution)/shard_map/pallas_call | solution.py:290
  35.1 0.7 %shard_map.77 = (f32[2,16,16]{2,1,0:T(8,128)}, f32[2,16,16]{2,1,0:T(8,128)}, f32[2,16,128]{2,1,0:T(8,128)}) custom-call(f32[3,16,128]{2,1,0:T(8,128)S(1)} %shard_map.76.packed_ref), custom_call_target="tpu_custom_call" | custom-call | tf_op jit(solution)/shard_map/pallas_call | solution.py:320

commit v2 on v1

--- a/solution.py
+++ b/solution.py
@@ -36,14 +36,15 @@
     return jnp.where(rows <= cols, scaled[:, :n], 0.0), scaled[:, n:]
 
 
-def pack(gram):
-    quarter = gram.shape[0] // 4
-    return jnp.concatenate([gram[i * quarter : (i + 1) * quarter] for i in range(4)], axis=1)
+def pack(blocks):
+    half = blocks[0].shape[0] // 2
+    return jnp.concatenate([block[h * half : (h + 1) * half] for block in blocks for h in range(2)], axis=1)
 
 
 def unpack(packed):
-    width = packed.shape[1] // 4
-    return jnp.concatenate([packed[:, i * width : (i + 1) * width] for i in range(4)], axis=0)
+    width = packed.shape[1] // 8
+    parts = [packed[:, i * width : (i + 1) * width] for i in range(8)]
+    return [jnp.concatenate(parts[2 * i : 2 * i + 2], axis=0) for i in range(4)]
 
 
 def partners(size, me):
@@ -60,13 +61,23 @@
     return pairs
 
 
+def others(size, me):
+    upper = 2 * me // size
+    order = []
+    for j in range(size - 1):
+        down = size - 1 - j - (me + j) // (size - 1)
+        up = j + 1 - (me + size - 1 - j) // size
+        order.append(down + upper * (up - down))
+    return order
+
+
 def kernel(
     nr, nc, group, total,
     rows_hbm, cols_hbm, counts_hbm, start_ref, blocks_ref,
     packed_ref,
-    tiles, weights, gat, xs, part, scat, ybuf, gsend, grow, gcol_send, gcol,
+    tiles, weights, gat, vbuf, xs, part, scat, ybuf, gsend, grow, gcol_send, gcol,
     rows_ref, cols_ref, counts_ref,
-    load_sem, row_send, row_recv, col_send, col_recv, gr_send, gr_recv, gc_send, gc_recv,
+    load_sem, row_send, row_recv, piece_recv, col_send, col_recv, gr_send, gr_recv, gc_send, gc_recv,
 ):
     me_r = lax.axis_index("row")
     me_c = lax.axis_index("col")
@@ -94,43 +105,45 @@
     loads[0].wait()
     pl.semaphore_wait(barrier, nr + nc - 2)
 
-    def spread_row(src, dst, send, recv, step):
+    pending = []
+    waits = list(range(nr - 2, nr // 2 - 1, -1)) + list(range(nr // 2))
+
+    def spread_row(src, dst, send, recv, step, peers, apart=False):
         copies = []
-        for d, (to, _) in enumerate(row_pairs):
+        for d, to in enumerate(peers):
             copy = pltpu.make_async_remote_copy(
                 src_ref=src, dst_ref=dst.at[me_r],
-                send_sem=send.at[step, d], recv_sem=recv.at[step, d],
+                send_sem=send.at[step], recv_sem=recv.at[d] if apart else recv.at[step],
                 device_id=(to, me_c), device_id_type=pl.DeviceIdType.MESH,
             )
             copy.start()
             copies.append(copy)
-        return copies
+        pending.append((dst.at[pl.ds(0, nr - 1)], send.at[step]))
+        return copies if apart else (dst.at[pl.ds(0, nr - 1)], recv.at[step])
 
     def spread_col(src, dst, send, recv, step, scatter):
-        copies = []
-        for d, (to, _) in enumerate(col_pairs):
+        for to, _ in col_pairs:
             copy = pltpu.make_async_remote_copy(
                 src_ref=src.at[to] if scatter else src, dst_ref=dst.at[me_c],
-                send_sem=send.at[step, d], recv_sem=recv.at[step, d],
+                send_sem=send.at[step], recv_sem=recv.at[step],
                 device_id=(me_r, to), device_id_type=pl.DeviceIdType.MESH,
             )
             copy.start()
-            copies.append(copy)
-        return copies
-
-    def received(copies):
-        for copy in copies:
-            copy.wait_recv()
+        pending.append((dst.at[pl.ds(0, nc - 1)], send.at[step]))
+        return dst.at[pl.ds(0, nc - 1)], recv.at[step]
+
+    def settled(like, sem):
+        pltpu.make_async_copy(like, like, sem).wait()
 
     def cat(value):
         return jnp.concatenate([value[p] for p in range(piece)], axis=1)
 
-    def mean_start(step, gram):
-        gsend[step] = pack(gram) * (1.0 / total)
-        return spread_row(gsend.at[step], grow.at[step], gr_send, gr_recv, step)
+    def mean_start(step, blocks):
+        gsend[step] = pack(blocks) * (1.0 / total)
+        return spread_row(gsend.at[step], grow.at[step], gr_send, gr_recv, step, [to for to, _ in row_pairs])
 
     def mean_row(step, copies):
-        received(copies)
+        settled(*copies)
         grow[step, pl.ds(me_r, 1)] = gsend[step][None]
         value = grow[step, 0]
         for r in range(1, nr):
@@ -142,7 +155,7 @@
         return spread_col(gcol_send.at[step], gcol.at[step], gc_send, gc_recv, step, False)
 
     def mean_end(step, copies):
-        received(copies)
+        settled(*copies)
         gcol[step, pl.ds(me_c, 1)] = gcol_send[step][None]
         value = gcol[step, 0]
         for c in range(1, nc):
@@ -161,7 +174,7 @@
             live = s < count
             col = jnp.clip(lax.select(live, cols_ref[s], 0), 0, nr * piece - 1)
             row = lax.select(live, rows_ref[s], -1)
-            prod = lax.dot_general(xs[col], weights[s], NT, preferred_element_type=F32)
+            prod = lax.dot_general(xs[col], weights[s], NN, preferred_element_type=F32)
             prod = prod[:k, :orb] + prod[:k, orb:] + prod[k:, :orb]
             zero = jnp.zeros_like(prod)
             return [acc + lax.select(row == r, prod, zero) for r, acc in enumerate(accs)]
@@ -182,89 +195,80 @@
         return spread_col(part.at[step], scat.at[step], col_send, col_recv, step, True)
 
     def reduced(step, copies):
-        received(copies)
+        settled(*copies)
         own = part[step, me_c]
         for _, other in col_pairs:
             own = own + scat[step, other]
         return own
 
-    pending = []
-    first = spread_row(gat.at[0, me_r], gat.at[0], row_send, row_recv, 0)
-    pending += first
+    first = spread_row(gat.at[0, me_r], gat.at[0], row_send, row_recv, 0, others(nr, me_r))
     for load in loads[1:]:
         load.wait()
     count = counts_ref[0, 0]
 
     def split_tile(s, carry):
-        tile = tiles[s]
+        tile = tiles[s].T
         high = tile.astype(BF16)
-        weights[s, :orb] = high
-        weights[s, orb:] = (tile - high.astype(F32)).astype(BF16)
+        weights[s, :, :orb] = high
+        weights[s, :, orb:] = (tile - high.astype(F32)).astype(BF16)
         return carry
 
     lax.fori_loop(0, capacity, split_tile, 0, unroll=2)
     split_vectors(0, me_r)
-    for copy, (_, other) in list(zip(first, row_pairs))[::-1]:
-        copy.wait_recv()
+    settled(*first)
+    for _, other in row_pairs:
         split_vectors(0, other)
     scatter0 = operate(0)
-    pending += scatter0
     s_all = jnp.concatenate([gat[0, r, p] for r in range(nr) for p in range(piece)], axis=1)
     ss = dot(s_all, s_all, NT)
-    ss = jnp.concatenate([ss, ss], axis=1)
-    middle_s = mean_column(0, pack(jnp.concatenate([ss, ss], axis=0)) * (1.0 / total))
-    pending += middle_s
+    middle_s = mean_column(0, pack([ss] * 4) * (1.0 / total))
     y_raw = reduced(0, scatter0)
     ybuf[...] = y_raw
     gat[1, pl.ds(me_r, 1)] = y_raw[None]
-    second = spread_row(ybuf, gat.at[1], row_send, row_recv, 1)
-    pending += second
-    _, inv0 = factor(mean_end(0, middle_s)[:k, :k])
-    v1 = dot(inv0, cat(gat[0, me_r]))
+    second = spread_row(ybuf, gat.at[1], row_send, piece_recv, 1, [to for to, _ in row_pairs], True)
+    _, inv0 = factor(mean_end(0, middle_s)[0])
     hv1 = dot(inv0, cat(y_raw))
-
-    def gram_of(q, left, right):
+    v_all = dot(inv0, s_all)
+    for r in range(nr):
+        vbuf[r] = v_all[:, r * piece * orb : (r + 1) * piece * orb]
+    v1 = vbuf[me_r]
+
+    def gram_of(left, right):
         both = jnp.concatenate([left, right], axis=0)
         return dot(both, both, NT)
 
     split_vectors(1, me_r)
-    both = gram_of(me_r, v1, hv1)
-    for copy, (_, other) in list(zip(second, row_pairs))[::-1]:
-        left = dot(inv0, cat(gat[0, other]))
-        copy.wait_recv()
+    both = gram_of(v1, hv1)
+    for d in waits:
+        other = row_pairs[d][1]
+        second[d].wait_recv()
         split_vectors(1, other)
-        both = both + gram_of(other, left, dot(inv0, cat(gat[1, other])))
-    middle0 = mean_column(1, pack(both) * (1.0 / total))
-    pending += middle0
+        both = both + gram_of(vbuf[other], dot(inv0, cat(gat[1, other])))
+    middle0 = mean_column(1, pack([both[:k, :k], both[:k, k:], both[k:, k:], both[k:, k:]]) * (1.0 / total))
     scatter1 = operate(1)
-    pending += scatter1
-    gram = mean_end(1, middle0)
-    q1, alpha1, yy1 = gram[:k, :k], gram[:k, k:], gram[k:, k:]
-    beta1, inv1 = factor(yy1 - dot(alpha1, alpha1, TN) - dot(alpha1, alpha1 - dot(q1, alpha1), TN))
-    v2 = dot(inv1, hv1 - dot(alpha1, v1, TN))
+    q1, alpha1, yy1, _ = mean_end(1, middle0)
+    w1 = hv1 - dot(alpha1, v1, TN)
+    drift = dot(alpha1, hv1, TN)
+    beta1, inv1 = factor(yy1 - dot(alpha1, alpha1 + (alpha1 - dot(q1, alpha1)), TN))
+    v2 = dot(inv1, w1)
     known = dot(beta1, v1)
-    shift = dot(dot(inv1, alpha1, NT), hv1)
+    shift = dot(inv1, drift)
     lead = dot(inv1, inv0)
     y2 = dot(lead, cat(reduced(1, scatter1))) - shift
     w2 = y2 - known
     both = jnp.concatenate([v2, w2], axis=0)
     grams = dot(both, jnp.concatenate([both, y2], axis=0), NT)
-    top = grams[:k, : 2 * k]
-    low = jnp.concatenate([grams[:k, 2 * k :], grams[k:, k : 2 * k]], axis=1)
-    mean1 = mean_start(0, jnp.concatenate([top, low], axis=0))
-    pending += mean1
+    mean1 = mean_start(0, [grams[:k, :k], grams[:k, k : 2 * k], grams[:k, 2 * k :], grams[k:, k : 2 * k]])
     middle1 = mean_column(2, mean_row(0, mean1))
-    pending += middle1
-    gram = mean_end(2, middle1)
-    qq, pw, alpha2, ww = gram[:k, :k], gram[:k, k:], gram[k:, :k], gram[k:, k:]
+    qq, pw, alpha2, ww = mean_end(2, middle1)
     rest = pw - dot(qq, alpha2)
     beta2, inv2 = factor(ww - dot(pw, alpha2, TN) - dot(alpha2, rest, TN))
     out = dot(inv2, w2 - dot(alpha2, v2, TN))
     for p in range(piece):
         packed_ref[p, :, :orb] = out[:, p * orb : (p + 1) * orb]
     packed_ref[piece, :, : 4 * k] = jnp.concatenate([alpha1, alpha2, beta1, beta2], axis=1)
-    for copy in pending:
-        copy.wait_send()
+    for like, sem in pending:
+        settled(like, sem)
 
 
 def finish(packed_ref, alphas_ref, betas_ref, next_ref):
@@ -286,7 +290,7 @@
     vmem = pl.BlockSpec(memory_space=pltpu.VMEM)
     dma = pltpu.SemaphoreType.DMA
     width = 4 * 2 * k
-    height = 2 * k // 4
+    height = k // 2
     packed = pl.pallas_call(
         functools.partial(kernel, nr, nc, group, total),
         out_shape=pltpu.VMEM((piece + 1, k, orb), F32),
@@ -294,8 +298,9 @@
         out_specs=vmem,
         scratch_shapes=[
             pltpu.VMEM((capacity, orb, orb), F32),
-            pltpu.VMEM((capacity, 2 * orb, orb), BF16),
+            pltpu.VMEM((capacity, orb, 2 * orb), BF16),
             pltpu.VMEM((2, nr, piece, k, orb), F32),
+            pltpu.VMEM((nr, k, piece * orb), F32),
             pltpu.VMEM((nr * piece, 2 * k, orb), BF16),
             pltpu.VMEM((2, nc, piece, k, orb), F32),
             pltpu.VMEM((2, nc, piece, k, orb), F32),
@@ -308,10 +313,10 @@
             pltpu.SMEM((capacity,), jnp.int32),
             pltpu.SMEM((1, 1), jnp.int32),
             dma((5,)),
-            dma((2, nr)), dma((2, nr)),
-            dma((2, nc)), dma((2, nc)),
-            dma((1, nr)), dma((1, nr)),
-            dma((3, nc)), dma((3, nc)),
+            dma((2,)), dma((1,)), dma((nr - 1,)),
+            dma((2,)), dma((2,)),
+            dma((1,)), dma((1,)),
+            dma((3,)), dma((3,)),
         ],
         compiler_params=pltpu.CompilerParams(
             collective_id=0, has_side_effects=True, vmem_limit_bytes=56 << 20

time: 36.1 us -> 34 us (0.942)
  Pallas kernels: 34.5 us -> 32.5 us
    pallas_call x1, Pallas kernels: 33.8 us -> 31.8 us  [on_device(): pl.pallas_call(functools.partial(kernel, nr, nc, group, total), out_shape...]
where the time goes in v2:
time: 34 us; the launch traced here: 33.8 us
  Pallas kernels  32.5 us (96%)
  between operations  1.29 us (4%)
    pallas_call x1, Pallas kernels, on_device(): pl.pallas_call(functools.partial(kernel, nr, nc, group, total), out_shape...  31.8 us
    pallas_call x1, Pallas kernels, on_device(): pl.pallas_call(finish, out_shape=(jax.ShapeDtypeStruct((2, k, k), F32), j...  0.69 us

profile of v2, /device:TPU:0, one launch (start us, length us, event | category | flops | bytes accessed | tf_op | source)
XLA Modules:
  0.0 33.8 jit_solution(11273439037501332428)
XLA Ops:
  1.3 31.8 %shard_map.76.packed_ref = f32[3,16,128]{2,1,0:T(8,128)S(1)} custom-call(s32[58]{0:T(128)} %bitcast.4, s32[58]{0:T(128)} %bitcast.5, s32[1,1]{1,0:T(1,128)S(6)} %copy.8.counts_hbm, f32[2,16,128]{2,1,0:T(8,128)} %start_ref.1, f32[58,128,128]{2,1,0:T(8,128)} %bitcast.3), custom_call_target="tpu_custom_call" | custom-call | tf_op jit(solution)/shard_map/pallas_call | solution.py:294
  33.1 0.7 %shard_map.77 = (f32[2,16,16]{2,1,0:T(8,128)}, f32[2,16,16]{2,1,0:T(8,128)}, f32[2,16,128]{2,1,0:T(8,128)}) custom-call(f32[3,16,128]{2,1,0:T(8,128)S(1)} %shard_map.76.packed_ref), custom_call_target="tpu_custom_call" | custom-call | tf_op jit(solution)/shard_map/pallas_call | solution.py:325

commit v3 on v2

--- a/solution.py
+++ b/solution.py
@@ -17,6 +17,14 @@
 
 def dot(left, right, dims=NN):
     return lax.dot_general(left, right, dims, precision=HIGHEST, preferred_element_type=F32)
+
+
+def small(left, right):
+    n = left.shape[0]
+    terms = [jnp.broadcast_to(left[:, j : j + 1], (n, n)) * right[j : j + 1] for j in range(n)]
+    while len(terms) > 1:
+        terms = [terms[i] + terms[i + 1] for i in range(0, len(terms) - 1, 2)] + terms[len(terms) - len(terms) % 2 :]
+    return terms[0]
 
 
 def factor(gram):
@@ -247,13 +255,14 @@
     middle0 = mean_column(1, pack([both[:k, :k], both[:k, k:], both[k:, k:], both[k:, k:]]) * (1.0 / total))
     scatter1 = operate(1)
     q1, alpha1, yy1, _ = mean_end(1, middle0)
-    w1 = hv1 - dot(alpha1, v1, TN)
-    drift = dot(alpha1, hv1, TN)
-    beta1, inv1 = factor(yy1 - dot(alpha1, alpha1 + (alpha1 - dot(q1, alpha1)), TN))
+    turned1 = alpha1.T
+    beta1, inv1 = factor(yy1 - small(turned1, alpha1 + (alpha1 - small(q1, alpha1))))
+    w1 = hv1 - dot(turned1, v1)
+    drift = dot(turned1, hv1)
     v2 = dot(inv1, w1)
     known = dot(beta1, v1)
     shift = dot(inv1, drift)
-    lead = dot(inv1, inv0)
+    lead = small(inv1, inv0)
     y2 = dot(lead, cat(reduced(1, scatter1))) - shift
     w2 = y2 - known
     both = jnp.concatenate([v2, w2], axis=0)
@@ -261,9 +270,10 @@
     mean1 = mean_start(0, [grams[:k, :k], grams[:k, k : 2 * k], grams[:k, 2 * k :], grams[k:, k : 2 * k]])
     middle1 = mean_column(2, mean_row(0, mean1))
     qq, pw, alpha2, ww = mean_end(2, middle1)
-    rest = pw - dot(qq, alpha2)
-    beta2, inv2 = factor(ww - dot(pw, alpha2, TN) - dot(alpha2, rest, TN))
-    out = dot(inv2, w2 - dot(alpha2, v2, TN))
+    turned2 = alpha2.T
+    rest = pw - small(qq, alpha2)
+    beta2, inv2 = factor(ww - small(pw.T, alpha2) - small(turned2, rest))
+    out = dot(inv2, w2 - dot(turned2, v2))
     for p in range(piece):
         packed_ref[p, :, :orb] = out[:, p * orb : (p + 1) * orb]
     packed_ref[piece, :, : 4 * k] = jnp.concatenate([alpha1, alpha2, beta1, beta2], axis=1)

time: 34 us -> 33.6 us (0.988)
  Pallas kernels: 32.5 us -> 32.1 us
    pallas_call x1, Pallas kernels: 31.8 us -> 31.4 us  [on_device(): pl.pallas_call(functools.partial(kernel, nr, nc, group, total), out_shape...]
where the time goes in v3:
time: 33.6 us; the launch traced here: 33.4 us
  Pallas kernels  32.1 us (96%)
  between operations  1.29 us (4%)
    pallas_call x1, Pallas kernels, on_device(): pl.pallas_call(functools.partial(kernel, nr, nc, group, total), out_shape...  31.4 us
    pallas_call x1, Pallas kernels, on_device(): pl.pallas_call(finish, out_shape=(jax.ShapeDtypeStruct((2, k, k), F32), j...  0.69 us

profile of v3, /device:TPU:0, one launch (start us, length us, event | category | flops | bytes accessed | tf_op | source)
XLA Modules:
  0.0 33.4 jit_solution(7463292932716822834)
XLA Ops:
  1.3 31.4 %shard_map.76.packed_ref = f32[3,16,128]{2,1,0:T(8,128)S(1)} custom-call(s32[58]{0:T(128)} %bitcast.4, s32[58]{0:T(128)} %bitcast.5, s32[1,1]{1,0:T(1,128)S(6)} %copy.8.counts_hbm, f32[2,16,128]{2,1,0:T(8,128)} %start_ref.1, f32[58,128,128]{2,1,0:T(8,128)} %bitcast.3), custom_call_target="tpu_custom_call" | custom-call | tf_op jit(solution)/shard_map/pallas_call | solution.py:304
  32.7 0.7 %shard_map.77 = (f32[2,16,16]{2,1,0:T(8,128)}, f32[2,16,16]{2,1,0:T(8,128)}, f32[2,16,128]{2,1,0:T(8,128)}) custom-call(f32[3,16,128]{2,1,0:T(8,128)S(1)} %shard_map.76.packed_ref), custom_call_target="tpu_custom_call" | custom-call | tf_op jit(solution)/shard_map/pallas_call | solution.py:335
